TPU v7x, 512 devices: a whole 4x8x8 slice. The times are simulated.
512 devices in a mesh: row: 32 (over z_lo, y), col: 16 (over z_hi, x, core).
Axes of the slice: x: 4, y: 8, z: 8 (z_hi: 2, z_lo: 4; z = z_hi * 4 + z_lo), core: 2. Of those that a mesh axis runs over, the one named last changes fastest.
Arguments:
- tiles: bfloat16 [16384, 2, 8192], P('row', None, 'col'), may hold values from -0.078125 to 0.078125
- energy: float32 [16384], P(('row', 'col')), may hold values from 0.5 to 8
- vectors: float32 [16, 16384], P(None, ('row', 'col')), may hold values from -6 to 6
- previous: float32 [16, 16384], P(None, ('row', 'col')), may hold values from -6 to 6
- coefs: float32 [2, 3, 16, 16], replicated, may hold values from -0.875 to 0.875
- irrep_of_unit: int32 [256], replicated, may hold values from 0 to 63, never falling along the last dimension, each value on 1 to 8 neighbouring positions
- coupled: int32 [64, 64], replicated, may hold values 0 or 1
Outputs:
- field: float32 [16, 16384], P(None, ('row', 'col'))
- search: float32 [16, 16384], P(None, ('row', 'col'))
- thetas: float32 [2, 16], replicated
Inputs may be any that keep to these rules, and one draw needn't show every extreme that they name: `irrep_of_unit`: never falls along the units; each irrep is a run of 1 to 8 units, and some irrep has exactly 8.
All inputs are finite; a program needn't handle non-finite values.
Results may differ from a plain program's by a relative error of at most 0.0011.
Values may be sent and summed in bfloat16 or wider, within the bound.
A program may use at most 64 MiB of HBM per device.

v0:
```python
import jax
import jax.numpy as jnp
from jax import lax
from jax.sharding import PartitionSpec as P

ITERS = 2
UNIT = 64


def spread_2(block, axis, holder):
    block = jnp.where(lax.axis_index(axis) == holder, block, jnp.zeros_like(block))
    return lax.psum(block, axis)


def body(tiles, energy, vectors, previous, coefs, irrep_of_unit, coupled):
    col_count = lax.axis_size("col")
    row_count = lax.axis_size("row")
    grid_row = lax.axis_index("row")
    grid_col = lax.axis_index("col")
    seg_rows = tiles.shape[0]
    seg_units = seg_rows // UNIT
    piece_len = vectors.shape[1]
    order_total = row_count * seg_rows
    labels = jnp.arange(coupled.shape[0], dtype=jnp.int32)
    row_ids = lax.dynamic_slice_in_dim(irrep_of_unit, grid_row * seg_units, seg_units, 0)
    row_hot = (row_ids[:, None] == labels[None, :]).astype(jnp.float32)
    row_couple = jnp.dot(row_hot, coupled.astype(jnp.float32))
    rows_global = grid_row * seg_rows + jnp.arange(seg_rows, dtype=jnp.int32)
    masked_list = []
    for which_half in range(2):
        block_index = which_half * col_count + grid_col
        col_ids = lax.dynamic_slice_in_dim(irrep_of_unit, block_index * seg_units, seg_units, 0)
        col_hot = (col_ids[:, None] == labels[None, :]).astype(jnp.float32)
        unit_mask = jnp.dot(row_couple, col_hot.T)
        full_mask = jnp.broadcast_to(
            unit_mask[:, None, :, None], (seg_units, UNIT, seg_units, UNIT)
        ).reshape(seg_rows, seg_rows)
        cols_global = block_index * seg_rows + jnp.arange(seg_rows, dtype=jnp.int32)
        lower = cols_global[None, :] <= rows_global[:, None]
        keep = jnp.where(lower & (full_mask > 0.5), 1.0, 0.0).astype(jnp.bfloat16)
        masked_list.append(tiles[:, which_half, :] * keep)
    masked = jnp.stack(masked_list)
    own_half = grid_row // col_count

    def apply_ham(current):
        narrow = current.astype(jnp.bfloat16)
        segment_row = lax.all_gather(narrow, "col", axis=1, tiled=True)
        whole = lax.all_gather(segment_row, "row", axis=1, tiled=True)
        col_segs = [
            lax.dynamic_slice_in_dim(
                whole, (which_half * col_count + grid_col) * seg_rows, seg_rows, 1
            )
            for which_half in range(2)
        ]
        direct = jnp.einsum("kc,rc->kr", col_segs[0], masked[0], preferred_element_type=jnp.float32)
        direct = direct + jnp.einsum(
            "kc,rc->kr", col_segs[1], masked[1], preferred_element_type=jnp.float32
        )
        row_part = lax.psum_scatter(direct, "col", scatter_dimension=1, tiled=True)
        transposed = jnp.einsum(
            "kr,hrc->hkc", segment_row, masked, preferred_element_type=jnp.float32
        )
        col_total = lax.psum(transposed, "row")
        picked = lax.dynamic_index_in_dim(col_total, own_half, 0, keepdims=False)
        mirrored = spread_2(picked, "col", grid_row % col_count)
        col_part = lax.dynamic_slice_in_dim(mirrored, grid_col * piece_len, piece_len, 1)
        return row_part + col_part + energy[None, :] * current

    field = vectors
    search = previous
    quotients = []
    high = lax.Precision.HIGHEST
    for iteration in range(ITERS):
        image = apply_ham(field)
        self_dot, cross = lax.psum(
            (jnp.sum(field * field, axis=1), jnp.sum(field * image, axis=1)), ("row", "col")
        )
        theta = cross / self_dot
        resid = image - theta[:, None] * field
        spread = lax.psum(jnp.sum(resid * resid, axis=1), ("row", "col"))
        scaled = resid * lax.rsqrt(spread / order_total + 1e-06)[:, None]
        new_search = jnp.dot(coefs[iteration, 1].T, scaled, precision=high) + jnp.dot(
            coefs[iteration, 2].T, search, precision=high
        )
        field = jnp.dot(coefs[iteration, 0].T, field, precision=high) + new_search
        search = new_search
        quotients.append(theta)
    return (field, search, jnp.stack(quotients))


def solution(mesh):
    placed = (
        P("row", None, "col"),
        P(("row", "col")),
        P(None, ("row", "col")),
        P(None, ("row", "col")),
        P(),
        P(),
        P(),
    )
    return jax.shard_map(
        body,
        mesh=mesh,
        in_specs=placed,
        out_specs=(P(None, ("row", "col")), P(None, ("row", "col")), P()),
        check_vma=False,
    )
```

profile of v0, /device:TPU:1, one launch (start us, length us, event | category | flops | bytes accessed | tf_op | source)
XLA Modules:
  0.0 1349.4 jit_solution(3365493604088614180)
XLA Ops:
  8.1 0.9 fusion.41
  9.0 0.9 fusion.6
  10.3 3.4 fusion.40
  13.8 36.4 %all-gather = bf16[16,32,16]{1,2,0:T(8,128)(2,1)S(1)} all-gather(bf16[1,32,16]{1,2,0:T(8,128)(2,1)S(1)} %convert_bitcast_fusion.1), channel_id=1, replica_groups=mesh['row'=32,'col'=16] {'col'}, dimensions={0}, use_global_device_ids=true | all-gather | bytes 17408 | tf_op jit(solution)/shard_map/all_gather | solution.py:47
  51.3 1.4 gt.39
  52.8 72.9 %all_gather.13 = bf16[16,16384]{1,0:T(8,128)(2,1)} all-gather(bf16[16,512]{1,0:T(8,128)(2,1)S(1)} %bitcast.89), channel_id=1, replica_groups=mesh['row'=32,'col'=16] {'row'}, dimensions={1}, use_global_device_ids=true | all-gather | bytes 540672 | tf_op jit(solution)/shard_map/all_gather | solution.py:48
  125.7 1.6 fusion.3
  128.1 0.9 fusion.12
  129.1 1.0 convolution_add_fusion.1
  130.1 0.9 copy.21
  134.0 0.9 convolution_bitcast_fusion.1
  134.9 80.0 %reduce-scatter.7.cloned.1.call-done = f32[32,16]{1,0:T(8,128)} async-done(((f32[512,16]{1,0:T(8,128)}), f32[32,16]{1,0:T(8,128)}) %reduce-scatter.7.cloned.1.call-update) | async-done | bytes 2064
  215.7 177.0 %all-reduce.5.cloned.1.call-done = f32[2,16,512]{2,1,0:T(8,128)} async-done(((f32[2,16,512]{2,1,0:T(8,128)}), f32[2,16,512]{2,1,0:T(8,128)}) %all-reduce.5.cloned.1.call-update) | async-done | bytes 65552 | tf_op jit(solution)/shard_map/psum | solution.py:63
  393.5 96.7 %psum.71 = f32[16,512]{1,0:T(8,128)S(1)} all-reduce(f32[16,512]{1,0:T(8,128)S(1)} %select_bitcast_fusion.1), channel_id=1, replica_groups=mesh['row'=32,'col'=16] {'col'}, use_global_device_ids=true, to_apply=%region_2.3 | all-reduce | flops 8192 | bytes 65536 | tf_op jit(solution)/shard_map/psum | solution.py:12
  490.3 100.6 %all-reduce.1 = (f32[16]{0:T(128)S(1)}, f32[16]{0:T(128)S(1)}) all-reduce(f32[16]{0:T(128)S(1)} %get-tuple-element.6, f32[16]{0:T(128)S(1)} %get-tuple-element.5), channel_id=1, replica_groups=mesh['row'=32,'col'=16] {'row','col'}, use_global_device_ids=true, to_apply=%region_4.5 | all-reduce | flops 32 | bytes 256 | tf_op jit(solution)/shard_map/psum | solution.py:75
  591.1 95.5 %psum.74 = f32[16]{0:T(128)S(1)} all-reduce(f32[16]{0:T(128)S(1)} %get-tuple-element.13), channel_id=1, replica_groups=mesh['row'=32,'col'=16] {'row','col'}, use_global_device_ids=true, to_apply=%region_8.9 | all-reduce | flops 16 | bytes 128 | tf_op jit(solution)/shard_map/psum | solution.py:80
  687.3 29.6 %all-gather.1 = bf16[16,32,16]{1,2,0:T(8,128)(2,1)S(1)} all-gather(bf16[1,32,16]{1,2,0:T(8,128)(2,1)S(1)} %convert_bitcast_fusion), channel_id=1, replica_groups=mesh['row'=32,'col'=16] {'col'}, dimensions={0}, use_global_device_ids=true | all-gather | bytes 17408 | tf_op jit(solution)/shard_map/all_gather | solution.py:47
  717.1 63.2 %all_gather.15 = bf16[16,16384]{1,0:T(8,128)(2,1)S(1)} all-gather(bf16[16,512]{1,0:T(8,128)(2,1)S(1)} %bitcast.88), channel_id=1, replica_groups=mesh['row'=32,'col'=16] {'row'}, dimensions={1}, use_global_device_ids=true | all-gather | bytes 540672 | tf_op jit(solution)/shard_map/all_gather | solution.py:48
  781.7 0.9 convolution_bitcast_fusion
  782.6 86.6 %reduce-scatter.9.cloned.1.call-done = f32[32,16]{1,0:T(8,128)} async-done(((f32[512,16]{1,0:T(8,128)}), f32[32,16]{1,0:T(8,128)}) %reduce-scatter.9.cloned.1.call-update) | async-done | bytes 2064
  870.0 176.3 %all-reduce.7.cloned.1.call-done = f32[2,16,512]{2,1,0:T(8,128)} async-done(((f32[2,16,512]{2,1,0:T(8,128)}), f32[2,16,512]{2,1,0:T(8,128)}) %all-reduce.7.cloned.1.call-update) | async-done | bytes 65552 | tf_op jit(solution)/shard_map/psum | solution.py:63
  1047.0 96.7 %psum.76 = f32[16,512]{1,0:T(8,128)S(1)} all-reduce(f32[16,512]{1,0:T(8,128)S(1)} %select_bitcast_fusion), channel_id=1, replica_groups=mesh['row'=32,'col'=16] {'col'}, use_global_device_ids=true, to_apply=%region_11.12 | all-reduce | flops 8192 | bytes 65536 | tf_op jit(solution)/shard_map/psum | solution.py:12
  1143.9 100.6 %all-reduce = (f32[16]{0:T(128)S(1)}, f32[16]{0:T(128)S(1)}) all-reduce(f32[16]{0:T(128)S(1)} %get-tuple-element.4, f32[16]{0:T(128)S(1)} %get-tuple-element.3), channel_id=1, replica_groups=mesh['row'=32,'col'=16] {'row','col'}, use_global_device_ids=true, to_apply=%region_13.14 | all-reduce | flops 32 | bytes 256 | tf_op jit(solution)/shard_map/psum | solution.py:75
  1244.7 95.5 %psum.79 = f32[16]{0:T(128)S(1)} all-reduce(f32[16]{0:T(128)S(1)} %get-tuple-element.11), channel_id=1, replica_groups=mesh['row'=32,'col'=16] {'row','col'}, use_global_device_ids=true, to_apply=%region_17.18 | all-reduce | flops 16 | bytes 128 | tf_op jit(solution)/shard_map/psum | solution.py:80
  (70 shorter events, 13.4 us)
Async XLA Ops:
  8.0 678.8 %copy-start = (f32[16,32]{1,0:T(8,128)S(1)}, f32[16,32]{1,0:T(8,128)}, u32[]{:S(2)}) copy-start(f32[16,32]{1,0:T(8,128)} %param.10) | copy-start | bytes 6148
  8.0 206.9 %reduce-scatter.7.cloned.1.call-start = ((), (), s32[]{:S(2)}) async-start(), calls=%async_computation.4 | async-start | bytes 278528
  10.3 3.5 copy-start.7
  127.3 0.8 copy-start.3
  127.4 1.7 copy-start.1
  130.9 261.8 %all-reduce.5.cloned.1.call-start = ((), (), s32[]{:S(2)}) async-start(), calls=%async_computation.2 | async-start | bytes 131072 | tf_op jit(solution)/shard_map/psum | solution.py:63
  133.1 0.8 copy-start.5
  133.1 357.0 %copy-start.8 = (f32[32]{0:T(128)S(1)}, f32[32]{0:T(128)}, u32[]{:S(2)}) copy-start(f32[32]{0:T(128)} %param.8) | copy-start | bytes 388
  133.2 553.5 %copy-start.9 = (f32[2,3,16,16]{3,2,1,0:T(8,128)S(1)}, f32[2,3,16,16]{3,2,1,0:T(8,128)}, u32[]{:S(2)}) copy-start(f32[2,3,16,16]{3,2,1,0:T(8,128)} %param.11) | copy-start | bytes 18436
  134.8 645.5 %copy-start.4 = (bf16[512,512]{1,0:T(8,128)(2,1)S(1)}, bf16[512,512]{1,0:T(8,128)(2,1)}, u32[]{:S(2)}) copy-start(bf16[512,512]{1,0:T(8,128)(2,1)} %copy-done.3) | copy-start | bytes 1572868
  134.8 645.7 %copy-start.2 = (bf16[512,512]{1,0:T(8,128)(2,1)S(1)}, bf16[512,512]{1,0:T(8,128)(2,1)}, u32[]{:S(2)}) copy-start(bf16[512,512]{1,0:T(8,128)(2,1)} %copy-done.1) | copy-start | bytes 1572868
  134.9 734.4 %reduce-scatter.9.cloned.1.call-start = ((), (), s32[]{:S(2)}) async-start(), calls=%async_computation.5 | async-start | bytes 278528
  717.1 64.6 %copy-start.6 = (bf16[1,512,512]{2,1,0:T(8,128)(2,1)S(1)}, bf16[1,512,512]{2,1,0:T(8,128)(2,1)}, u32[]{:S(2)}) copy-start(bf16[1,512,512]{2,1,0:T(8,128)(2,1)} %copy-done.5) | copy-start | bytes 1572868
  781.7 264.6 %all-reduce.7.cloned.1.call-start = ((), (), s32[]{:S(2)}) async-start(), calls=%async_computation.3 | async-start | bytes 131072 | tf_op jit(solution)/shard_map/psum | solution.py:63
  1340.6 1.4 copy-start.10
Sparse Core Ops, SparseCore 0:
  131.1 83.8 reduce-scatter.6
  781.8 87.4 reduce-scatter.8
Sparse Core Ops, SparseCore 1:
  134.9 257.7 all-reduce.4
  785.1 261.2 all-reduce.6
where the time goes:
time: 1350 us
  blocking collectives  788 us (58%)
  waiting for transfers between devices  520 us (39%)
  between operations  15.7 us (1%)
  local copies, waits for them, and re-layouts  13.5 us (1%)
    psum x2, waiting for transfers between devices, apply_ham(): col_total = lax.psum(transposed, 'row')  353 us
    psum x2, blocking collectives, body(): lax.psum((jnp.sum(field * field, axis=1), jnp.sum(field * image, axis=1))...  201 us
    psum x2, blocking collectives, spread_2(): return lax.psum(block, axis)  193 us
    psum x2, blocking collectives, body(): spread = lax.psum(jnp.sum(resid * resid, axis=1), ('row', 'col'))  191 us
    unnamed x6, waiting for transfers between devices  167 us
    all_gather x2, blocking collectives, apply_ham(): whole = lax.all_gather(segment_row, 'row', axis=1, tiled=True)  136 us
    all_gather x2, blocking collectives, apply_ham(): segment_row = lax.all_gather(narrow, 'col', axis=1, tiled=True)  66 us
  transfers between devices with their start and end apart: 4, of which 4 were waited for; matrix products, arithmetic and copies ran while one was open for 0% of the time, Pallas kernels for 0%

commit v1 on v0

v1 whole, which is shorter than its diff:
```python
import jax
import jax.numpy as jnp
from jax import lax
from jax.experimental import pallas as pl
from jax.experimental.pallas import tpu as pltpu
from jax.sharding import PartitionSpec as P

MESH = pl.DeviceIdType.MESH
UNIT = 64
ROWS = 32
COLS = 16
SEG = 512
NVEC = 16
LANES = 128
GROUP = 4
TINY = 1e-37


def remote(src, dst, send, recv, row, col):
    return pltpu.make_async_remote_copy(
        src_ref=src, dst_ref=dst, send_sem=send, recv_sem=recv, device_id=(row, col), device_id_type=MESH
    )


def wait_all(ref, sem):
    pltpu.make_async_copy(ref, ref, sem).wait()


def segment_of(ref):
    tiles = []
    for t in range(SEG // LANES):
        tiles.append(jnp.concatenate([ref[4 * t + g] for g in range(GROUP)], axis=0))
    return jnp.concatenate(tiles, axis=1)


def store_pieces(ref, value):
    for t in range(value.shape[1] // LANES):
        for g in range(GROUP):
            ref[4 * t + g] = value[4 * g : 4 * g + 4, LANES * t : LANES * (t + 1)]


def mixed(mix, field, scaled, search):
    rest = jnp.zeros((LANES - 3 * NVEC, field.shape[1]), jnp.float32)
    stack = jnp.concatenate([field, scaled, search, rest], axis=0)
    return jnp.dot(mix, stack, precision=lax.Precision.HIGHEST, preferred_element_type=jnp.float32)


def kernel(
    own_ref, masked_ref, mix_ref,
    field_out, search_out, theta_out,
    group_buf, field_piece, search_piece, next_piece,
    field_row, field_col, search_row, search_col, image_row, image_col, last_row,
    direct_out, mirror_out, sums, sums_next, image_piece, image_next,
    stat_out, stats, stats_next, field_next,
    group_send, group_recv,
    field_send, field_recv, search_send, search_recv, image_send, image_recv, last_send, last_recv,
    sums_send, sums_recv, stat_send, stat_recv,
):
    row = lax.axis_index("row")
    col = lax.axis_index("col")
    tile = col // GROUP
    lane_group = col % GROUP
    home = lax.rem(row, COLS)
    half = row // COLS
    on_diag = home == col
    depth = (col // 8) * 4 + row // 8
    inner = lax.rem(col, 8)

    def stat_peer(index, sign):
        step = (index // 8 - 1) * sign
        there = lax.rem(depth + step + 8, 8)
        return lax.rem(there, 4) * 8 + lax.rem(index, 8), (there // 4) * 8 + inner

    def is_self(r, c):
        return jnp.logical_and(r == row, c == col)

    barrier = pltpu.get_barrier_semaphore()

    def greet(r, c):
        @pl.when(jnp.logical_not(is_self(r, c)))
        def _():
            pl.semaphore_signal(barrier, inc=1, device_id=(r, c), device_id_type=MESH)

    def greet_32(k, carry):
        greet(k, home)
        greet(lax.rem(k, 2) * COLS + col, k // 2)
        greet(*stat_peer(k, -1))
        return carry

    def greet_16(k, carry):
        greet(row, k)
        return carry

    lax.fori_loop(0, ROWS, greet_32, 0)
    lax.fori_loop(0, COLS, greet_16, 0)
    pl.semaphore_wait(barrier, 15 + 31 + 64 - 2 * on_diag.astype(jnp.int32))

    def put(src, dst, send, recv, r, c):
        mine = is_self(r, c)

        @pl.when(jnp.logical_not(mine))
        def _():
            remote(src, dst, send, recv, r, c).start()

        @pl.when(mine)
        def _():
            pltpu.make_async_copy(src, dst, recv).start()

    def group_put(k, carry):
        put(own_ref, group_buf.at[lane_group], group_send, group_recv, row, GROUP * tile + k)
        return carry

    lax.fori_loop(0, GROUP, group_put, 0)
    wait_all(group_buf, group_recv)
    own = (group_buf[0] + group_buf[1]) + (group_buf[2] + group_buf[3])
    field_t = own[0:16]
    search_t = own[16:32]
    energy = own[32:33]
    store_pieces(field_piece, field_t)
    store_pieces(search_piece, search_t)

    def row_put(src, dst, send, recv):
        def step(k, carry):
            put(src, dst.at[col], send, recv, row, k)
            return carry

        lax.fori_loop(0, COLS, step, 0)

    def col_put(src, dst, send, recv):
        def step(k, carry):
            put(src, dst.at[half, col], send, recv, lax.rem(row + k, ROWS), home)
            return carry

        lax.fori_loop(0, ROWS, step, 0)

    col_put(field_piece.at[lane_group], field_col, field_send.at[0], field_recv.at[0])
    row_put(field_piece.at[lane_group], field_row, field_send.at[1], field_recv.at[1])
    col_put(search_piece.at[lane_group], search_col, search_send.at[0], search_recv.at[0])
    row_put(search_piece.at[lane_group], search_row, search_send.at[1], search_recv.at[1])

    def multiply(narrow_row, narrow_cols, out_sums, which):
        direct = jnp.zeros((NVEC, SEG), jnp.float32)
        for h in range(2):
            block = masked_ref[h]
            mirror = jnp.dot(narrow_row, block, preferred_element_type=jnp.float32)
            store_pieces(mirror_out.at[which, h], mirror)
            direct = direct + lax.dot_general(
                narrow_cols[h], block, (((1,), (1,)), ((), ())), preferred_element_type=jnp.float32
            )
        store_pieces(direct_out.at[which], direct)

        def mirror_put(k, carry):
            h = k // COLS
            j = lax.rem(k, COLS)
            put(mirror_out.at[which, h, j], out_sums.at[COLS + row], sums_send.at[which, 0], sums_recv.at[which], COLS * h + col, j)
            return carry

        def direct_put(k, carry):
            put(direct_out.at[which, k], out_sums.at[col], sums_send.at[which, 1], sums_recv.at[which], row, k)
            return carry

        lax.fori_loop(0, 2 * COLS, mirror_put, 0)
        lax.fori_loop(0, COLS, direct_put, 0)

    sub = lax.broadcasted_iota(jnp.int32, (NVEC, LANES), 0)
    lane = lax.broadcasted_iota(jnp.int32, (NVEC, LANES), 1)
    eye = sub == lane

    def to_lanes(column):
        return jnp.sum(jnp.where(eye, column, 0.0), axis=0, keepdims=True)

    def to_column(lanes):
        return jnp.sum(jnp.where(eye, lanes, 0.0), axis=1, keepdims=True)

    def share_stats(field, image, dst, which):
        self_dot = jnp.sum(field * field, axis=1, keepdims=True)
        cross = jnp.sum(field * image, axis=1, keepdims=True)
        usable = self_dot > TINY
        local = jnp.where(usable, cross / jnp.where(usable, self_dot, 1.0), 0.0)
        left = image - local * field
        spread = jnp.sum(left * left, axis=1, keepdims=True)
        for i, value in enumerate((self_dot, cross, spread, local)):
            stat_out[which, i : i + 1, :] = to_lanes(value)

        def step(k, carry):
            r, c = stat_peer(k, 1)
            put(stat_out.at[which], dst.at[row], stat_send.at[which], stat_recv.at[which], r, c)
            return carry

        lax.fori_loop(0, ROWS, step, 0)

    def merge_stats(src, which):
        wait_all(src, stat_recv.at[which])
        self_i, cross_i, spread_i, local_i = [src[:, i, :] for i in range(4)]
        self_dot = jnp.sum(self_i, axis=0, keepdims=True)
        cross = jnp.sum(cross_i, axis=0, keepdims=True)
        theta = cross / jnp.where(lane[0:1] < NVEC, self_dot, 1.0)
        away = local_i - theta
        spread = jnp.sum(spread_i + self_i * away * away, axis=0, keepdims=True)
        scale = lax.rsqrt(spread / (ROWS * SEG) + 1e-06)
        theta_out[which : which + 1, :] = theta[:, :NVEC]
        return to_column(theta), to_column(scale)

    wait_all(field_row, field_recv.at[1])
    field_r = segment_of(field_row)
    wait_all(field_col, field_recv.at[0])
    field_c = [segment_of(field_col.at[h]) for h in range(2)]
    multiply(field_r.astype(jnp.bfloat16), [x.astype(jnp.bfloat16) for x in field_c], sums, 0)

    wait_all(search_row, search_recv.at[1])
    wait_all(search_col, search_recv.at[0])
    wait_all(sums, sums_recv.at[0])
    image_piece[...] = jnp.sum(sums[...], axis=0) + energy * field_piece[lane_group]
    row_put(image_piece, image_row, image_send.at[1], image_recv.at[1])
    col_put(image_piece, image_col, image_send.at[0], image_recv.at[0])
    wait_all(image_row, image_recv.at[1])
    field_r = segment_of(field_row)
    image_r = segment_of(image_row)
    share_stats(field_r, image_r, stats, 0)
    wait_all(image_col, image_recv.at[0])
    theta, scale = merge_stats(stats, 0)

    images = [image_r] + [segment_of(image_col.at[h]) for h in range(2)]
    fields = [field_r] + [segment_of(field_col.at[h]) for h in range(2)]
    searches = [segment_of(search_row)] + [segment_of(search_col.at[h]) for h in range(2)]
    narrow = []
    for i in range(3):
        scaled = (images[i] - theta * fields[i]) * scale
        following = mixed(mix_ref[0, 0:NVEC], fields[i], scaled, searches[i])
        if i == 0:
            field_next[...] = following
        narrow.append(following.astype(jnp.bfloat16))
    multiply(narrow[0], narrow[1:], sums_next, 1)
    image_t = jnp.concatenate([image_row[GROUP * tile + g] for g in range(GROUP)], axis=0)
    scaled_t = (image_t - theta * field_t) * scale
    both = mixed(mix_ref[0], field_t, scaled_t, search_t)
    field_t, search_t = both[0:NVEC], both[NVEC:]
    store_pieces(next_piece, field_t)

    wait_all(sums_next, sums_recv.at[1])
    image_next[...] = jnp.sum(sums_next[...], axis=0) + energy * next_piece[lane_group]
    row_put(image_next, last_row, last_send, last_recv)
    wait_all(last_row, last_recv)
    share_stats(field_next[...], segment_of(last_row), stats_next, 1)
    theta, scale = merge_stats(stats_next, 1)
    image_t = jnp.concatenate([last_row[GROUP * tile + g] for g in range(GROUP)], axis=0)
    scaled_t = (image_t - theta * field_t) * scale
    both = mixed(mix_ref[1], field_t, scaled_t, search_t)
    field_t, search_t = both[0:NVEC], both[NVEC:]
    shift = lax.rem(LANES - (LANES // GROUP) * lane_group, LANES)
    field_out[...] = pltpu.roll(field_t, shift, 1)[:, : LANES // GROUP]
    search_out[...] = pltpu.roll(search_t, shift, 1)[:, : LANES // GROUP]

    wait_all(group_buf.at[pl.ds(0, GROUP - 1)], group_send)

    def drain(sem, ref, whole, diagonal):
        if not diagonal:
            wait_all(ref.at[pl.ds(0, whole)], sem)
        else:
            @pl.when(on_diag)
            def _():
                wait_all(ref.at[pl.ds(0, whole - 1)], sem)

            @pl.when(jnp.logical_not(on_diag))
            def _():
                wait_all(ref.at[pl.ds(0, whole)], sem)

    for sem in (field_send, search_send, image_send):
        drain(sem.at[0], sums, ROWS, True)
        drain(sem.at[1], sums, COLS - 1, False)
    drain(last_send, sums, COLS - 1, False)
    for which in range(2):
        drain(sums_send.at[which, 0], sums, 2 * COLS, True)
        drain(sums_send.at[which, 1], sums, COLS - 1, False)
        drain(stat_send.at[which], sums, ROWS - 1, False)


def body(tiles, energy, vectors, previous, coefs, irrep_of_unit, coupled):
    grid_row = lax.axis_index("row")
    grid_col = lax.axis_index("col")
    seg_units = SEG // UNIT
    labels = jnp.arange(coupled.shape[0], dtype=jnp.int32)
    row_ids = lax.dynamic_slice_in_dim(irrep_of_unit, grid_row * seg_units, seg_units, 0)
    row_hot = (row_ids[:, None] == labels[None, :]).astype(jnp.float32)
    row_couple = jnp.dot(row_hot, coupled.astype(jnp.float32))
    rows_global = grid_row * SEG + jnp.arange(SEG, dtype=jnp.int32)
    masked_list = []
    for which_half in range(2):
        block_index = which_half * COLS + grid_col
        col_ids = lax.dynamic_slice_in_dim(irrep_of_unit, block_index * seg_units, seg_units, 0)
        col_hot = (col_ids[:, None] == labels[None, :]).astype(jnp.float32)
        unit_mask = jnp.dot(row_couple, col_hot.T)
        full_mask = jnp.broadcast_to(
            unit_mask[:, None, :, None], (seg_units, UNIT, seg_units, UNIT)
        ).reshape(SEG, SEG)
        cols_global = block_index * SEG + jnp.arange(SEG, dtype=jnp.int32)
        lower = cols_global[None, :] <= rows_global[:, None]
        keep = jnp.where(lower & (full_mask > 0.5), 1.0, 0.0).astype(jnp.bfloat16)
        masked_list.append(tiles[:, which_half, :] * keep)
    masked = jnp.stack(masked_list)
    mine = jnp.concatenate([vectors, previous, jnp.broadcast_to(energy[None, :], (8, energy.shape[0]))], axis=0)
    place = (jnp.arange(LANES, dtype=jnp.int32) // (LANES // GROUP)) == grid_col % GROUP
    own = jnp.where(place[None, :], jnp.tile(mine, (1, GROUP)), 0.0)
    turned = jnp.swapaxes(coefs, 2, 3)
    search_rows = jnp.concatenate([jnp.zeros_like(turned[:, 0]), turned[:, 1], turned[:, 2]], axis=2)
    field_rows = jnp.concatenate([turned[:, 0], turned[:, 1], turned[:, 2]], axis=2)
    mixes = jnp.concatenate([field_rows, search_rows], axis=1)
    mixes = jnp.pad(mixes, ((0, 0), (0, 0), (0, LANES - 3 * NVEC)))

    f32 = jnp.float32
    dma = pltpu.SemaphoreType.DMA
    vmem = pl.BlockSpec(memory_space=pltpu.VMEM)
    piece = (GROUP, LANES)
    return pl.pallas_call(
        kernel,
        out_shape=(
            jax.ShapeDtypeStruct((NVEC, LANES // GROUP), f32),
            jax.ShapeDtypeStruct((NVEC, LANES // GROUP), f32),
            jax.ShapeDtypeStruct((2, NVEC), f32),
        ),
        in_specs=[vmem] * 3,
        out_specs=(vmem, vmem, vmem),
        scratch_shapes=[
            pltpu.VMEM((GROUP, 40, LANES), f32),
            pltpu.VMEM((GROUP, *piece), f32),
            pltpu.VMEM((GROUP, *piece), f32),
            pltpu.VMEM((GROUP, *piece), f32),
            pltpu.VMEM((COLS, *piece), f32),
            pltpu.VMEM((2, COLS, *piece), f32),
            pltpu.VMEM((COLS, *piece), f32),
            pltpu.VMEM((2, COLS, *piece), f32),
            pltpu.VMEM((COLS, *piece), f32),
            pltpu.VMEM((2, COLS, *piece), f32),
            pltpu.VMEM((COLS, *piece), f32),
            pltpu.VMEM((2, COLS, *piece), f32),
            pltpu.VMEM((2, 2, COLS, *piece), f32),
            pltpu.VMEM((COLS + ROWS, *piece), f32),
            pltpu.VMEM((COLS + ROWS, *piece), f32),
            pltpu.VMEM(piece, f32),
            pltpu.VMEM(piece, f32),
            pltpu.VMEM((2, *piece), f32),
            pltpu.VMEM((ROWS, *piece), f32),
            pltpu.VMEM((ROWS, *piece), f32),
            pltpu.VMEM((NVEC, SEG), f32),
            dma, dma,
            dma((2,)), dma((2,)), dma((2,)), dma((2,)), dma((2,)), dma((2,)), dma, dma,
            dma((2, 2)), dma((2,)), dma((2,)), dma((2,)),
        ],
        compiler_params=pltpu.CompilerParams(collective_id=0, has_side_effects=True),
        name="lobpcg",
    )(own, masked, mixes)


def solution(mesh):
    placed = (
        P("row", None, "col"),
        P(("row", "col")),
        P(None, ("row", "col")),
        P(None, ("row", "col")),
        P(),
        P(),
        P(),
    )
    return jax.shard_map(
        body,
        mesh=mesh,
        in_specs=placed,
        out_specs=(P(None, ("row", "col")), P(None, ("row", "col")), P()),
        check_vma=False,
    )
```

time: 1350 us -> 93.7 us (0.07)
  blocking collectives: 788 us -> 0 us
  waiting for transfers between devices: 520 us -> 0 us
  Pallas kernels: 0 us -> 81.3 us
  between operations: 15.7 us -> 0.84 us
    psum x6 -> x0, blocking collectives: 585 us -> none  [the longest x2 201 us: body(): lax.psum((jnp.sum(field * field, axis=1), jnp.sum(field * image, axis=1))...]
    psum x2 -> x0, waiting for transfers between devices: 353 us -> none  [apply_ham(): col_total = lax.psum(transposed, 'row')]
    all_gather x4 -> x0, blocking collectives: 202 us -> none  [the longest x2 136 us: apply_ham(): whole = lax.all_gather(segment_row, 'row', axis=1, tiled=True)]
    unnamed x6 -> x0, waiting for transfers between devices: 167 us -> none
    pallas_call x0 -> x1, Pallas kernels: none -> 81.3 us  [body(): pl.pallas_call(kernel, out_shape=(jax.ShapeDtypeStruct((NVEC, LANES // GR...]
  transfers between devices with their start and end apart: 4 -> 0, of which waited for: 4 -> 0; matrix products, arithmetic and copies ran while one was open for 0% -> 0% of each run, Pallas kernels for 0% -> 0%
where the time goes in v1:
time: 93.7 us; the launch traced here: 93.3 us
  Pallas kernels  81.3 us (87%)
  local copies, waits for them, and re-layouts  8.18 us (9%)
  other arithmetic  2.42 us (3%)
    pallas_call x1, Pallas kernels, body(): pl.pallas_call(kernel, out_shape=(jax.ShapeDtypeStruct((NVEC, LANES // GR...  81.3 us
    unnamed x22, local copies, waits for them, and re-layouts  4.06 us

profile of v1, /device:TPU:1, one launch (start us, length us, event | category | flops | bytes accessed | tf_op | source)
XLA Modules:
  0.0 93.3 jit_solution(10495986429272913224)
XLA Ops:
  0.7 0.7 copy-done.5
  1.3 0.1 fusion.9
  1.4 0.2 fusion.2
  1.6 0.2 convolution_compare_fusion.1
  1.8 0.2 broadcast_in_dim.29
  2.0 0.7 gt.29
  2.7 0.2 convolution_compare_fusion
  2.9 0.2 broadcast_in_dim.60
  3.1 0.7 gt.31
  3.8 1.5 %fusion.8 = (bf16[512,1,512]{2,1,0:T(2,128)(2,1)S(1)}, bf16[512,1,512]{2,1,0:T(2,128)(2,1)S(1)}) fusion(bf16[512,2,512]{2,1,0:T(2,128)(2,1)S(1)} %copy-done), kind=kLoop, calls=%fused_computation.31 | loop fusion | bytes 2097152 | tf_op jit(solution)/shard_map/slice | solution.py:299
  5.4 0.6 fusion
  6.0 1.1 %pad_maximum_fusion.masked_ref = bf16[2,512,512]{2,1,0:T(8,128)(2,1)} fusion(bf16[1,512,512]{2,1,0:T(8,128)(2,1)S(1)} %get-tuple-element.9, bf16[1,512,512]{2,1,0:T(8,128)(2,1)S(1)} %get-tuple-element.8), kind=kLoop, calls=%fused_computation.2 | loop fusion | flops 524288 | bytes 2097152 | tf_op jit(solution)/shard_map/stack | solution.py:300
  7.1 0.7 copy-done.3
  7.8 0.1 tile.10
  8.0 0.6 broadcast_select_fusion.own_ref
  8.6 0.1 copy-done.1
  8.6 0.1 copy.15
  8.7 0.1 maximum_maximum_fusion
  8.8 0.6 pad.4.mix_ref
  9.4 81.3 %lobpcg.1 = (f32[16,32]{1,0:T(8,128)}, f32[16,32]{1,0:T(8,128)}, f32[2,16]{1,0:T(2,128)}) custom-call(f32[40,128]{1,0:T(8,128)} %broadcast_select_fusion.own_ref, bf16[2,512,512]{2,1,0:T(8,128)(2,1)} %pad_maximum_fusion.masked_ref, f32[2,32,128]{2,1,0:T(8,128)} %pad.4.mix_ref), custom_call_target="tpu_custom_call" | custom-call | tf_op jit(solution)/shard_map/lobpcg/pallas_call | solution.py:314
  90.8 1.3 %copy.27 = f32[16,32]{1,0:T(8,128)} copy(f32[16,32]{1,0:T(8,128)} %get-tuple-element.18) | data formatting | bytes 4096
  92.1 0.6 copy.28
  92.7 0.1 copy-done.6
  92.7 0.6 copy.29
  (23 shorter events, 0.1 us)
Async XLA Ops:
  0.6 0.8 copy-start.8
  0.6 0.7 copy-start.5
  2.0 1.8 %copy-start = (bf16[512,2,512]{2,1,0:T(2,128)(2,1)S(1)}, bf16[512,2,512]{2,1,0:T(2,128)(2,1)}, u32[]{:S(2)}) copy-start(bf16[512,2,512]{2,1,0:T(2,128)(2,1)} %param.7) | copy-start | bytes 3145732
  6.0 1.1 %copy-start.7 = (f32[32]{0:T(128)S(1)}, f32[32]{0:T(128)}, u32[]{:S(2)}) copy-start(f32[32]{0:T(128)} %param.8) | copy-start | bytes 388
  7.1 0.7 copy-start.3
  7.1 0.7 copy-start.2
  7.8 0.8 copy-start.1
  90.8 1.3 %copy-start.4 = (f32[16,32]{1,0:T(8,128)S(1)}, f32[16,32]{1,0:T(8,128)}, u32[]{:S(2)}) copy-start(f32[16,32]{1,0:T(8,128)} %get-tuple-element.19) | copy-start | bytes 6148
  92.1 0.7 copy-start.6

commit v2 on v1

v2 whole, which is shorter than its diff:
```python
import jax
import jax.numpy as jnp
from jax import lax
from jax.experimental import pallas as pl
from jax.experimental.pallas import tpu as pltpu
from jax.sharding import PartitionSpec as P

MESH = pl.DeviceIdType.MESH
UNIT = 64
ROWS = 32
COLS = 16
SEG = 512
NVEC = 16
LANES = 128
GROUP = 4
QUARTER = LANES // GROUP
TINY = 1e-37


def remote(src, dst, send, recv, row, col):
    return pltpu.make_async_remote_copy(
        src_ref=src, dst_ref=dst, send_sem=send, recv_sem=recv, device_id=(row, col), device_id_type=MESH
    )


def wait_all(ref, sem):
    pltpu.make_async_copy(ref, ref, sem).wait()


def segment_of(ref):
    tiles = []
    for t in range(SEG // LANES):
        tiles.append(jnp.concatenate([ref[4 * t + g] for g in range(GROUP)], axis=0))
    return jnp.concatenate(tiles, axis=1)


def store_pieces(ref, value):
    for t in range(value.shape[1] // LANES):
        for g in range(GROUP):
            ref[4 * t + g] = value[4 * g : 4 * g + 4, LANES * t : LANES * (t + 1)]


def mixed(mix, field, scaled, search):
    rest = jnp.zeros((LANES - 3 * NVEC, field.shape[1]), jnp.float32)
    stack = jnp.concatenate([field, scaled, search, rest], axis=0)
    return jnp.dot(mix, stack, precision=lax.Precision.HIGHEST, preferred_element_type=jnp.float32)


def unpacked(ref):
    block = lax.broadcasted_iota(jnp.int32, (NVEC, LANES), 1) // QUARTER
    rows = []
    for b in range(GROUP):
        total = None
        for g in range(GROUP):
            part = jnp.concatenate([ref[4 * t + g] for t in range(GROUP)], axis=0)
            part = pltpu.roll(part, QUARTER * ((g - b) % GROUP), 1) if g != b else part
            total = part if total is None else jnp.where(block == g, part, total)
        rows.append(total)
    tiles = []
    for t in range(SEG // LANES):
        tiles.append(jnp.concatenate([rows[b][4 * t : 4 * t + 4] for b in range(GROUP)], axis=0))
    return jnp.concatenate(tiles, axis=1)


def kernel(
    tiles_hbm, energy_ref, vectors_ref, previous_ref, coefs_ref, irrep_ref, coupled_ref,
    out_ref,
    tiles_buf, masked, pad, mix_ref, energy_out, energy_buf,
    field_out, search_out, field_piece, next_piece, field_full,
    field_row, field_col, search_row, search_col, image_row, image_col, last_row,
    direct_out, mirror_out, sums, sums_next, image_piece, image_next,
    stat_out, near_stats, far_stats,
    tiles_sem, energy_send, energy_recv,
    field_send, field_recv, search_send, search_recv, image_send, image_recv, last_send, last_recv,
    sums_send, sums_recv, stat_send, stat_recv,
):
    row = lax.axis_index("row")
    col = lax.axis_index("col")
    tile = col // GROUP
    lane_group = lax.rem(col, GROUP)
    home = lax.rem(row, COLS)
    half = row // COLS
    on_diag = home == col
    low = row // 8
    y = lax.rem(row, 8)
    inner = lax.rem(col, 8)
    core = lax.rem(col, 2)
    depth = (col // 8) * 4 + low

    load_tiles = pltpu.make_async_copy(tiles_hbm, tiles_buf, tiles_sem)
    load_tiles.start()

    def near_peer(k):
        z = k // 2
        return lax.rem(z, 4) * 8 + y, (z // 4) * 8 + (inner // 2) * 2 + lax.rem(k, 2)

    def far_peer(k):
        return low * 8 + lax.rem(k, 8), (col // 8) * 8 + (k // 8) * 2 + core

    def is_self(r, c):
        return jnp.logical_and(r == row, c == col)

    barrier = pltpu.get_barrier_semaphore()

    def greet(r, c):
        @pl.when(jnp.logical_not(is_self(r, c)))
        def _():
            pl.semaphore_signal(barrier, inc=1, device_id=(r, c), device_id_type=MESH)

    def greet_sources(k, carry):
        greet(lax.rem(k, 2) * COLS + col, k // 2)
        return carry

    def greet_row(k, carry):
        greet(row, k)
        return carry

    lax.fori_loop(0, ROWS, greet_sources, 0)
    lax.fori_loop(0, COLS, greet_row, 0)

    pad[...] = jnp.zeros_like(pad)
    pad[0:16, 0:QUARTER] = vectors_ref[...]
    pad[16:32, 0:QUARTER] = previous_ref[...]
    pad[32:33, 0:QUARTER] = energy_ref[...]

    def packed(start):
        total = pad[start : start + 4]
        for b in range(1, GROUP):
            total = total + pltpu.roll(pad[start + 4 * b : start + 4 * b + 4], QUARTER * b, 1)
        return total

    field_out[...] = packed(0)
    search_out[...] = packed(16)
    energy_out[...] = pltpu.roll(pad[32:40], QUARTER * lane_group, 1)[0:1]

    pl.semaphore_wait(barrier, 15 + 32 - on_diag.astype(jnp.int32))

    def put(src, dst, send, recv, r, c):
        mine = is_self(r, c)

        @pl.when(jnp.logical_not(mine))
        def _():
            remote(src, dst, send, recv, r, c).start()

        @pl.when(mine)
        def _():
            pltpu.make_async_copy(src, dst, recv).start()

    def row_put(src, dst, send, recv):
        def step(k, carry):
            put(src, dst.at[col], send, recv, row, k)
            return carry

        lax.fori_loop(0, COLS, step, 0)

    def col_put(src, dst, send, recv):
        def step(k, carry):
            put(src, dst.at[half, col], send, recv, lax.rem(row + k, ROWS), home)
            return carry

        lax.fori_loop(0, ROWS, step, 0)

    col_put(field_out, field_col, field_send.at[0], field_recv.at[0])
    row_put(field_out, field_row, field_send.at[1], field_recv.at[1])

    def energy_put(k, carry):
        put(energy_out, energy_buf.at[lane_group], energy_send, energy_recv, row, GROUP * tile + k)
        return carry

    lax.fori_loop(0, GROUP, energy_put, 0)
    col_put(search_out, search_col, search_send.at[0], search_recv.at[0])
    row_put(search_out, search_row, search_send.at[1], search_recv.at[1])

    load_tiles.wait()
    strip_sub = lax.broadcasted_iota(jnp.int32, (UNIT, SEG), 0)
    strip_lane = lax.broadcasted_iota(jnp.int32, (UNIT, SEG), 1)
    unit_lane = lax.broadcasted_iota(jnp.int32, (1, SEG), 1) // UNIT

    def mask_strip(i, carry):
        mine = irrep_ref[row * (SEG // UNIT) + i]
        start = pl.multiple_of(i * UNIT, UNIT)
        for h in range(2):
            block = h * COLS + col
            allowed = jnp.zeros((1, SEG), jnp.int32)
            for j in range(SEG // UNIT):
                theirs = irrep_ref[block * (SEG // UNIT) + j]
                allowed = jnp.where(unit_lane == j, coupled_ref[mine, theirs], allowed)
            lower = strip_lane + block * SEG <= strip_sub + (row * SEG + start)
            keep = jnp.logical_and(lower, allowed > 0)
            strip = tiles_buf[pl.ds(start, UNIT), h, :].astype(jnp.float32)
            masked[h, pl.ds(start, UNIT), :] = jnp.where(keep, strip, 0.0).astype(jnp.bfloat16)
        return carry

    lax.fori_loop(0, SEG // UNIT, mask_strip, 0)

    mix_sub = lax.broadcasted_iota(jnp.int32, (LANES, LANES), 0)
    for i in range(2):
        mix_ref[i] = jnp.zeros((LANES, LANES), jnp.float32)
        for j in range(3):
            mix_ref[i, NVEC * j : NVEC * (j + 1), 0:NVEC] = coefs_ref[i, j]
        square = mix_ref[i]
        square = square + jnp.where(mix_sub >= NVEC, pltpu.roll(square, NVEC, 1), 0.0)
        mix_ref[i] = square.T

    def multiply(narrow_row, narrow_cols, out_sums, which):
        direct = jnp.zeros((NVEC, SEG), jnp.float32)
        for h in range(2):
            block = masked[h]
            mirror = jnp.dot(narrow_row, block, preferred_element_type=jnp.float32)
            store_pieces(mirror_out.at[which, h], mirror)
            direct = direct + lax.dot_general(
                narrow_cols[h], block, (((1,), (1,)), ((), ())), preferred_element_type=jnp.float32
            )
        store_pieces(direct_out.at[which], direct)

        def mirror_put(k, carry):
            h = k // COLS
            j = lax.rem(k, COLS)
            put(mirror_out.at[which, h, j], out_sums.at[COLS + row], sums_send.at[which, 0], sums_recv.at[which], COLS * h + col, j)
            return carry

        def direct_put(k, carry):
            put(direct_out.at[which, k], out_sums.at[col], sums_send.at[which, 1], sums_recv.at[which], row, k)
            return carry

        lax.fori_loop(0, 2 * COLS, mirror_put, 0)
        lax.fori_loop(0, COLS, direct_put, 0)

    sub = lax.broadcasted_iota(jnp.int32, (NVEC, LANES), 0)
    lane = lax.broadcasted_iota(jnp.int32, (NVEC, LANES), 1)
    eye = sub == lane
    eye_group = lane[0:GROUP] == sub[0:GROUP] + GROUP * lane_group

    def to_column(lanes):
        return jnp.sum(jnp.where(eye, lanes, 0.0), axis=1, keepdims=True)

    def quotient(cross, self_dot):
        usable = self_dot > TINY
        return jnp.where(usable, cross / jnp.where(usable, self_dot, 1.0), 0.0)

    def send_stats(rows, which, hop):
        for i, value in enumerate(rows):
            stat_out[which, hop, i : i + 1, :] = value
        src = stat_out.at[which, hop]

        def near_step(k, carry):
            put(src, near_stats.at[which, depth * 2 + core], stat_send.at[which, 0], stat_recv.at[which, 0], *near_peer(k))
            return carry

        def far_step(k, carry):
            put(src, far_stats.at[which, (inner // 2) * 8 + y], stat_send.at[which, 1], stat_recv.at[which, 1], *far_peer(k))
            return carry

        if hop == 0:
            lax.fori_loop(0, COLS, near_step, 0)
        else:
            lax.fori_loop(0, ROWS, far_step, 0)

    def share_stats(field, image, which):
        self_dot = jnp.sum(field * field, axis=1, keepdims=True)
        cross = jnp.sum(field * image, axis=1, keepdims=True)
        local = quotient(cross, self_dot)
        left = image - local * field
        spread = jnp.sum(left * left, axis=1, keepdims=True)
        rows = [
            jnp.sum(jnp.where(eye_group, value, 0.0), axis=0, keepdims=True)
            for value in (self_dot, cross, spread, local)
        ]
        send_stats(rows, which, 0)

    def merged(buf):
        self_i, cross_i, spread_i, local_i = [buf[:, i, :] for i in range(4)]
        self_dot = jnp.sum(self_i, axis=0, keepdims=True)
        cross = jnp.sum(cross_i, axis=0, keepdims=True)
        return self_i, spread_i, local_i, self_dot, cross

    def spread_about(self_i, spread_i, local_i, theta):
        away = local_i - theta
        return jnp.sum(spread_i + self_i * away * away, axis=0, keepdims=True)

    def relay_stats(which):
        buf = near_stats.at[which]
        wait_all(buf, stat_recv.at[which, 0])
        self_i, spread_i, local_i, self_dot, cross = merged(buf)
        local = quotient(cross, self_dot)
        send_stats([self_dot, cross, spread_about(self_i, spread_i, local_i, local), local], which, 1)

    def merge_stats(which):
        buf = far_stats.at[which]
        wait_all(buf, stat_recv.at[which, 1])
        self_i, spread_i, local_i, self_dot, cross = merged(buf)
        theta = cross / jnp.where(lane[0:1] < NVEC, self_dot, 1.0)
        spread = spread_about(self_i, spread_i, local_i, theta)
        scale = lax.rsqrt(spread / (ROWS * SEG) + 1e-06)
        out_ref[48 + which : 49 + which, :] = theta
        return to_column(theta), to_column(scale)

    def tile_of(ref):
        return jnp.concatenate([ref[GROUP * tile + g] for g in range(GROUP)], axis=0)

    def own_tile(ref):
        return ref[:, pl.ds(pl.multiple_of(tile * LANES, LANES), LANES)]

    wait_all(field_row, field_recv.at[1])
    field_r = unpacked(field_row)
    wait_all(field_col, field_recv.at[0])
    field_c = [unpacked(field_col.at[h]) for h in range(2)]
    multiply(field_r.astype(jnp.bfloat16), [x.astype(jnp.bfloat16) for x in field_c], sums, 0)
    fields = [field_r] + field_c
    for i in range(3):
        field_full[0, i] = fields[i]
    field_t = own_tile(field_full.at[0, 0])
    store_pieces(field_piece, field_t)
    wait_all(energy_buf, energy_recv)
    energy = (energy_buf[0] + energy_buf[1]) + (energy_buf[2] + energy_buf[3])
    wait_all(search_row, search_recv.at[1])
    wait_all(search_col, search_recv.at[0])
    searches = [unpacked(search_row)] + [unpacked(search_col.at[h]) for h in range(2)]
    for i in range(3):
        field_full[1, i] = searches[i]
    search_t = own_tile(field_full.at[1, 0])

    wait_all(sums, sums_recv.at[0])
    field_p = field_piece[lane_group]
    image_p = jnp.sum(sums[...], axis=0) + energy * field_p
    image_piece[...] = image_p
    share_stats(field_p, image_p, 0)
    col_put(image_piece, image_col, image_send.at[0], image_recv.at[0])
    row_put(image_piece, image_row, image_send.at[1], image_recv.at[1])
    relay_stats(0)
    wait_all(image_row, image_recv.at[1])
    wait_all(image_col, image_recv.at[0])
    theta, scale = merge_stats(0)

    images = [segment_of(image_row)] + [segment_of(image_col.at[h]) for h in range(2)]
    narrow = []
    for i in range(3):
        field_i = field_full[0, i]
        scaled = (images[i] - theta * field_i) * scale
        following = mixed(mix_ref[0, 0:NVEC], field_i, scaled, field_full[1, i])
        narrow.append(following.astype(jnp.bfloat16))
    multiply(narrow[0], narrow[1:], sums_next, 1)
    scaled_t = (tile_of(image_row) - theta * field_t) * scale
    both = mixed(mix_ref[0, 0 : 2 * NVEC], field_t, scaled_t, search_t)
    field_t, search_t = both[0:NVEC], both[NVEC:]
    store_pieces(next_piece, field_t)
    field_p = next_piece[lane_group]

    wait_all(sums_next, sums_recv.at[1])
    image_p = jnp.sum(sums_next[...], axis=0) + energy * field_p
    image_next[...] = image_p
    share_stats(field_p, image_p, 1)

    def last_put(k, carry):
        put(image_next, last_row.at[lane_group], last_send, last_recv, row, GROUP * tile + k)
        return carry

    lax.fori_loop(0, GROUP, last_put, 0)
    relay_stats(1)
    wait_all(last_row, last_recv)
    theta, scale = merge_stats(1)
    image_t = jnp.concatenate([last_row[g] for g in range(GROUP)], axis=0)
    scaled_t = (image_t - theta * field_t) * scale
    out_ref[0:48, :] = mixed_parts(mix_ref[1, 0 : 2 * NVEC], field_t, scaled_t, search_t, lane_group)

    def drain(sem, ref, whole, diagonal):
        if not diagonal:
            wait_all(ref.at[pl.ds(0, whole)], sem)
        else:
            @pl.when(on_diag)
            def _():
                wait_all(ref.at[pl.ds(0, whole - 1)], sem)

            @pl.when(jnp.logical_not(on_diag))
            def _():
                wait_all(ref.at[pl.ds(0, whole)], sem)

    drain(energy_send, energy_buf, GROUP - 1, False)
    drain(last_send, sums, GROUP - 1, False)
    for sem in (field_send, search_send, image_send):
        drain(sem.at[0], sums, ROWS, True)
        drain(sem.at[1], sums, COLS - 1, False)
    for which in range(2):
        drain(sums_send.at[which, 0], sums, 2 * COLS, True)
        drain(sums_send.at[which, 1], sums, COLS - 1, False)
        drain(stat_send.at[which, 0], sums, COLS - 1, False)
        drain(stat_send.at[which, 1], sums, ROWS - 1, False)


def mixed_parts(mix, field, scaled, search, lane_group):
    both = mixed(mix, field, scaled, search)
    both = pltpu.roll(both, lax.rem(LANES - QUARTER * lane_group, LANES), 1)
    return jnp.concatenate([both, jnp.zeros((NVEC, LANES), jnp.float32)], axis=0)


def split_out(all_ref, field_ref, search_ref, theta_ref):
    field_ref[...] = all_ref[0:NVEC, 0:QUARTER]
    search_ref[...] = all_ref[NVEC : 2 * NVEC, 0:QUARTER]
    theta_ref[...] = all_ref[48:50, 0:NVEC]


def body(tiles, energy, vectors, previous, coefs, irrep_of_unit, coupled):
    f32 = jnp.float32
    dma = pltpu.SemaphoreType.DMA
    vmem = pl.BlockSpec(memory_space=pltpu.VMEM)
    smem = pl.BlockSpec(memory_space=pltpu.SMEM)
    piece = (GROUP, LANES)
    everything = pl.pallas_call(
        kernel,
        out_shape=jax.ShapeDtypeStruct((56, LANES), f32),
        in_specs=[pl.BlockSpec(memory_space=pl.ANY), vmem, vmem, vmem, vmem, smem, smem],
        out_specs=vmem,
        scratch_shapes=[
            pltpu.VMEM((SEG, 2, SEG), jnp.bfloat16),
            pltpu.VMEM((2, SEG, SEG), jnp.bfloat16),
            pltpu.VMEM((40, LANES), f32),
            pltpu.VMEM((2, LANES, LANES), f32),
            pltpu.VMEM((1, LANES), f32),
            pltpu.VMEM((GROUP, 1, LANES), f32),
            pltpu.VMEM(piece, f32),
            pltpu.VMEM(piece, f32),
            pltpu.VMEM((GROUP, *piece), f32),
            pltpu.VMEM((GROUP, *piece), f32),
            pltpu.VMEM((2, 3, NVEC, SEG), f32),
            pltpu.VMEM((COLS, *piece), f32),
            pltpu.VMEM((2, COLS, *piece), f32),
            pltpu.VMEM((COLS, *piece), f32),
            pltpu.VMEM((2, COLS, *piece), f32),
            pltpu.VMEM((COLS, *piece), f32),
            pltpu.VMEM((2, COLS, *piece), f32),
            pltpu.VMEM((GROUP, *piece), f32),
            pltpu.VMEM((2, COLS, *piece), f32),
            pltpu.VMEM((2, 2, COLS, *piece), f32),
            pltpu.VMEM((COLS + ROWS, *piece), f32),
            pltpu.VMEM((COLS + ROWS, *piece), f32),
            pltpu.VMEM(piece, f32),
            pltpu.VMEM(piece, f32),
            pltpu.VMEM((2, 2, *piece), f32),
            pltpu.VMEM((2, COLS, *piece), f32),
            pltpu.VMEM((2, ROWS, *piece), f32),
            dma, dma, dma,
            dma((2,)), dma((2,)), dma((2,)), dma((2,)), dma((2,)), dma((2,)), dma, dma,
            dma((2, 2)), dma((2,)), dma((2, 2)), dma((2, 2)),
        ],
        compiler_params=pltpu.CompilerParams(collective_id=0, has_side_effects=True),
        name="lobpcg",
    )(tiles, energy[None, :], vectors, previous, coefs, irrep_of_unit, coupled)
    return pl.pallas_call(
        split_out,
        out_shape=(
            jax.ShapeDtypeStruct((NVEC, QUARTER), f32),
            jax.ShapeDtypeStruct((NVEC, QUARTER), f32),
            jax.ShapeDtypeStruct((2, NVEC), f32),
        ),
        in_specs=[vmem],
        out_specs=(vmem, vmem, vmem),
        name="split",
    )(everything)


def solution(mesh):
    placed = (
        P("row", None, "col"),
        P(("row", "col")),
        P(None, ("row", "col")),
        P(None, ("row", "col")),
        P(),
        P(),
        P(),
    )
    return jax.shard_map(
        body,
        mesh=mesh,
        in_specs=placed,
        out_specs=(P(None, ("row", "col")), P(None, ("row", "col")), P()),
        check_vma=False,
    )
```

time: 93.7 us -> 77.1 us (0.82)
  local copies, waits for them, and re-layouts: 8.18 us -> 0 us
  Pallas kernels: 81.3 us -> 76.2 us
  other arithmetic: 2.42 us -> 0 us
    pallas_call x1 -> x2, Pallas kernels: 81.3 us -> 76.2 us  [the longest x1 74.9 us: body(): pl.pallas_call(kernel, out_shape=jax.ShapeDtypeStruct((56, LANES), f32),...]
    unnamed x22 -> x0, local copies, waits for them, and re-layouts: 4.06 us -> none
    slice x1 -> x0, local copies, waits for them, and re-layouts: 1.5 us -> none  [body(): masked_list.append(tiles[:, which_half, :] * keep)]
    gt x2 -> x0, local copies, waits for them, and re-layouts: 1.37 us -> none  [body(): keep = jnp.where(lower & (full_mask > 0.5), 1.0, 0.0).astype(jnp.bfloat16)]
    another operation x1 -> x0, other arithmetic: 1.08 us -> none  [body(): masked = jnp.stack(masked_list)]
where the time goes in v2:
time: 77.1 us; the launch traced here: 76.9 us
  Pallas kernels  76.2 us (99%)
    pallas_call x1, Pallas kernels, body(): pl.pallas_call(kernel, out_shape=jax.ShapeDtypeStruct((56, LANES), f32),...  74.9 us

profile of v2, /device:TPU:1, one launch (start us, length us, event | category | flops | bytes accessed | tf_op | source)
XLA Modules:
  0.0 76.9 jit_solution(15461603502602742409)
XLA Ops:
  0.6 74.9 %lobpcg.1.all_ref = f32[56,128]{1,0:T(8,128)} custom-call(bf16[512,2,512]{2,1,0:T(2,128)(2,1)} %tiles_hbm.1, f32[1,32]{1,0:T(1,128)} %bitcast.1, f32[16,32]{1,0:T(8,128)} %vectors_ref.1, f32[16,32]{1,0:T(8,128)} %previous_ref.1, f32[2,3,16,16]{3,2,1,0:T(8,128)} %coefs_ref.1, s32[256]{0:T(256)} %irrep_ref.1, s32[64,64]{1,0:T(8,128)} %coupled_ref.1), custom_call_target="tpu_custom_call" | custom-call | tf_op jit(solution)/shard_map/lobpcg/pallas_call | solution.py:408
  75.5 1.4 %split.1 = (f32[16,32]{1,0:T(8,128)}, f32[16,32]{1,0:T(8,128)}, f32[2,16]{1,0:T(2,128)}) custom-call(f32[56,128]{1,0:T(8,128)} %lobpcg.1.all_ref), custom_call_target="tpu_custom_call" | custom-call | tf_op jit(solution)/shard_map/split/pallas_call | solution.py:448

commit v3 on v2

v3 whole, which is shorter than its diff:
```python
import jax
import jax.numpy as jnp
from jax import lax
from jax.experimental import pallas as pl
from jax.experimental.pallas import tpu as pltpu
from jax.sharding import PartitionSpec as P

MESH = pl.DeviceIdType.MESH
UNIT = 64
ROWS = 32
COLS = 16
SEG = 512
NVEC = 16
LANES = 128
GROUP = 4
QUARTER = LANES // GROUP
TINY = 1e-37


def remote(src, dst, send, recv, row, col):
    return pltpu.make_async_remote_copy(
        src_ref=src, dst_ref=dst, send_sem=send, recv_sem=recv, device_id=(row, col), device_id_type=MESH
    )


def wait_all(ref, sem):
    pltpu.make_async_copy(ref, ref, sem).wait()


def lane_block():
    return lax.broadcasted_iota(jnp.int32, (NVEC, LANES), 1) // QUARTER


def swapped(parts):
    block = lane_block()
    results = []
    for o in range(GROUP):
        total = None
        for i in range(GROUP):
            part = pltpu.roll(parts[i], QUARTER * ((i - o) % GROUP), 1) if i != o else parts[i]
            total = part if total is None else jnp.where(block == i, part, total)
        results.append(total)
    return results


def unpacked(ref, start=0):
    take = slice(start, start + GROUP)
    parts = [jnp.concatenate([ref[4 * t + g, take] for t in range(GROUP)], axis=0) for g in range(GROUP)]
    rows = swapped(parts)
    tiles = []
    for t in range(GROUP):
        tiles.append(jnp.concatenate([rows[b][4 * t : 4 * t + 4] for b in range(GROUP)], axis=0))
    return jnp.concatenate(tiles, axis=1)


def store_packed(ref, value):
    parts = []
    for b in range(GROUP):
        rows = [value[4 * b : 4 * b + 4, LANES * t : LANES * (t + 1)] for t in range(GROUP)]
        parts.append(jnp.concatenate(rows, axis=0))
    pieces = swapped(parts)
    for t in range(GROUP):
        for g in range(GROUP):
            ref[4 * t + g] = pieces[g][4 * t : 4 * t + 4]


def pack_own(value):
    total = value[0:4]
    for b in range(1, GROUP):
        total = total + pltpu.roll(value[4 * b : 4 * b + 4], QUARTER * b, 1)
    return total


def unpack_own(piece):
    rows = [piece] + [pltpu.roll(piece, LANES - QUARTER * b, 1) for b in range(1, GROUP)]
    return jnp.where(lane_block() == 0, jnp.concatenate(rows, axis=0), 0.0)


def mixed(mix, parts):
    totals = []
    for place, part in parts:
        total = None
        for k in range(NVEC):
            column = mix[:, NVEC * place + k : NVEC * place + k + 1]
            term = column * part[k : k + 1, :]
            total = term if total is None else total + term
        totals.append(total)
    result = totals[0]
    for total in totals[1:]:
        result = result + total
    return result


def kernel(
    tiles_hbm, energy_hbm, vectors_hbm, previous_hbm, coefs_hbm, irrep_hbm, coupled_hbm,
    out_ref,
    vectors_ref, previous_ref, energy_ref, coefs_ref, irrep_ref, coupled_ref, tiles_buf, masked, pad, mix_ref, field_out, image_out,
    field_row, field_col, image_row, image_col,
    direct_out, mirror_out, sums, stat_out, near_stats, far_stats,
    tiles_sem, load_sem, vec_send, vec_recv, sums_send, sums_recv, stat_send, stat_recv,
):
    row = lax.axis_index("row")
    col = lax.axis_index("col")
    home = lax.rem(row, COLS)
    half = row // COLS
    on_diag = home == col
    low = row // 8
    y = lax.rem(row, 8)
    inner = lax.rem(col, 8)
    core = lax.rem(col, 2)
    depth = (col // 8) * 4 + low

    def near_peer(k):
        z = k // 2
        return lax.rem(z, 4) * 8 + y, (z // 4) * 8 + (inner // 2) * 2 + lax.rem(k, 2)

    def far_peer(k):
        return low * 8 + lax.rem(k, 8), (col // 8) * 8 + (k // 8) * 2 + core

    def is_self(r, c):
        return jnp.logical_and(r == row, c == col)

    barrier = pltpu.get_barrier_semaphore()

    def greet(r, c):
        @pl.when(jnp.logical_not(is_self(r, c)))
        def _():
            pl.semaphore_signal(barrier, inc=1, device_id=(r, c), device_id_type=MESH)

    def greet_partners(k, carry):
        greet(lax.rem(k, 2) * COLS + col, k // 2)
        greet(k, home)
        return carry

    def greet_row(k, carry):
        greet(row, k)
        return carry

    lax.fori_loop(0, ROWS, greet_partners, 0)
    lax.fori_loop(0, COLS, greet_row, 0)

    loads = []
    for i, (src, dst) in enumerate((
        (vectors_hbm, vectors_ref), (previous_hbm, previous_ref), (energy_hbm, energy_ref),
        (irrep_hbm, irrep_ref), (coupled_hbm, coupled_ref), (coefs_hbm, coefs_ref),
    )):
        loads.append(pltpu.make_async_copy(src, dst, load_sem.at[i]))
        loads[-1].start()
    load_tiles = pltpu.make_async_copy(tiles_hbm, tiles_buf, tiles_sem)
    load_tiles.start()
    for load in loads:
        load.wait()

    pad[...] = jnp.zeros_like(pad)
    pad[0:16, 0:QUARTER] = vectors_ref[...]
    pad[16:32, 0:QUARTER] = previous_ref[...]
    pad[32:33, 0:QUARTER] = energy_ref[...]
    field_own = pad[0:16]
    search_own = pad[16:32]
    energy = pad[32:33]
    field_out[...] = pack_own(field_own)

    load_tiles.wait()
    strip_sub = lax.broadcasted_iota(jnp.int32, (UNIT, SEG), 0)
    strip_lane = lax.broadcasted_iota(jnp.int32, (UNIT, SEG), 1)
    unit_lane = lax.broadcasted_iota(jnp.int32, (1, SEG), 1) // UNIT

    def mask_strip(i, carry):
        mine = irrep_ref[row * (SEG // UNIT) + i]
        start = pl.multiple_of(i * UNIT, UNIT)
        for h in range(2):
            block = h * COLS + col
            allowed = jnp.zeros((1, SEG), jnp.int32)
            for j in range(SEG // UNIT):
                theirs = irrep_ref[block * (SEG // UNIT) + j]
                allowed = jnp.where(unit_lane == j, coupled_ref[mine, theirs], allowed)
            lower = strip_lane + block * SEG <= strip_sub + (row * SEG + start)
            keep = jnp.logical_and(lower, allowed > 0)
            strip = tiles_buf[pl.ds(start, UNIT), h, :].astype(jnp.float32)
            masked[h, pl.ds(start, UNIT), :] = jnp.where(keep, strip, 0.0).astype(jnp.bfloat16)
        return carry

    lax.fori_loop(0, SEG // UNIT, mask_strip, 0)

    for i in range(2):
        mix_ref[i] = jnp.zeros((LANES, LANES), jnp.float32)
        for j in range(3):
            mix_ref[i, NVEC * j : NVEC * (j + 1), 0:NVEC] = coefs_ref[i, j]
        square = mix_ref[i]
        mix_ref[i] = square.T

    pl.semaphore_wait(barrier, 15 + 64 - 2 * on_diag.astype(jnp.int32))

    def put(src, dst, send, recv, r, c):
        mine = is_self(r, c)

        @pl.when(jnp.logical_not(mine))
        def _():
            remote(src, dst, send, recv, r, c).start()

        @pl.when(mine)
        def _():
            pltpu.make_async_copy(src, dst, recv).start()

    def row_put(src, dst, send, recv):
        def step(k, carry):
            put(src, dst.at[col], send, recv, row, k)
            return carry

        lax.fori_loop(0, COLS, step, 0)

    def col_put(src, dst, send, recv):
        def step(k, carry):
            away = lax.rem(118891828 >> (4 * (k // 4)), 8)
            there = lax.rem(low + lax.rem(k, 4), 4) * 8 + lax.rem(y + away, 8)
            put(src, dst.at[half, col], send, recv, there, home)
            return carry

        lax.fori_loop(0, ROWS, step, 0)

    row_put(field_out, field_row, vec_send.at[0, 1], vec_recv.at[0, 1])
    col_put(field_out, field_col, vec_send.at[0, 0], vec_recv.at[0, 0])
    image_out[GROUP:] = pack_own(mixed(mix_ref[0, 0:NVEC], [(0, field_own), (2, search_own)]))
    energy_part = pack_own(energy * field_own)

    def mirror_products(vectors, which):
        narrow = vectors.astype(jnp.bfloat16)
        for h in range(2):
            mirror = jnp.dot(narrow, masked[h], preferred_element_type=jnp.float32)
            store_packed(mirror_out.at[which, h], mirror)

            def mirror_put(k, carry):
                j = lax.rem(k + row, COLS)
                put(mirror_out.at[which, h, j], sums.at[which, COLS + row], sums_send.at[which, 0], sums_recv.at[which], COLS * h + col, j)
                return carry

            lax.fori_loop(0, COLS, mirror_put, 0)

    def direct_products(vectors, which):
        direct = jnp.zeros((NVEC, SEG), jnp.float32)
        for h in range(2):
            narrow = vectors[h].astype(jnp.bfloat16)
            direct = direct + lax.dot_general(
                narrow, masked[h], (((1,), (1,)), ((), ())), preferred_element_type=jnp.float32
            )
        store_packed(direct_out.at[which], direct)

        def direct_put(k, carry):
            j = lax.rem(k + col, COLS)
            put(direct_out.at[which, j], sums.at[which, col], sums_send.at[which, 1], sums_recv.at[which], row, j)
            return carry

        lax.fori_loop(0, COLS, direct_put, 0)

    def summed(which):
        buf = sums.at[which]
        wait_all(buf, sums_recv.at[which])
        return jnp.sum(buf[...], axis=0)

    sub = lax.broadcasted_iota(jnp.int32, (NVEC, LANES), 0)
    lane = lax.broadcasted_iota(jnp.int32, (NVEC, LANES), 1)
    eye = sub == lane

    def to_column(lanes):
        return jnp.sum(jnp.where(eye, lanes, 0.0), axis=1, keepdims=True)

    def quotient(cross, self_dot):
        usable = self_dot > TINY
        return jnp.where(usable, cross / jnp.where(usable, self_dot, 1.0), 0.0)

    def send_stats(rows, which, hop):
        for i, value in enumerate(rows):
            stat_out[which, hop, i : i + 1, :] = value
        src = stat_out.at[which, hop]

        def near_step(k, carry):
            put(src, near_stats.at[which, depth * 2 + core], stat_send.at[which, 0], stat_recv.at[which, 0], *near_peer(k))
            return carry

        def far_step(k, carry):
            put(src, far_stats.at[which, (inner // 2) * 8 + y], stat_send.at[which, 1], stat_recv.at[which, 1], *far_peer(k))
            return carry

        if hop == 0:
            lax.fori_loop(0, COLS, near_step, 0)
        else:
            lax.fori_loop(0, ROWS, far_step, 0)

    def share_stats(field, image, which):
        self_dot = jnp.sum(field * field, axis=1, keepdims=True)
        cross = jnp.sum(field * image, axis=1, keepdims=True)
        local = quotient(cross, self_dot)
        left = image - local * field
        spread = jnp.sum(left * left, axis=1, keepdims=True)
        rows = [
            jnp.sum(jnp.where(eye, value, 0.0), axis=0, keepdims=True)
            for value in (self_dot, cross, spread, local)
        ]
        send_stats(rows, which, 0)

    def merged(buf):
        self_i, cross_i, spread_i, local_i = [buf[:, i, :] for i in range(4)]
        self_dot = jnp.sum(self_i, axis=0, keepdims=True)
        cross = jnp.sum(cross_i, axis=0, keepdims=True)
        return self_i, spread_i, local_i, self_dot, cross

    def spread_about(self_i, spread_i, local_i, theta):
        away = local_i - theta
        return jnp.sum(spread_i + self_i * away * away, axis=0, keepdims=True)

    def relay_stats(which):
        buf = near_stats.at[which]
        wait_all(buf, stat_recv.at[which, 0])
        self_i, spread_i, local_i, self_dot, cross = merged(buf)
        local = quotient(cross, self_dot)
        send_stats([self_dot, cross, spread_about(self_i, spread_i, local_i, local), local], which, 1)

    def merge_stats(which):
        buf = far_stats.at[which]
        wait_all(buf, stat_recv.at[which, 1])
        self_i, spread_i, local_i, self_dot, cross = merged(buf)
        theta = cross / jnp.where(lane[0:1] < NVEC, self_dot, 1.0)
        spread = spread_about(self_i, spread_i, local_i, theta)
        scale = lax.rsqrt(spread / (ROWS * SEG) + 1e-06)
        out_ref[32 + which : 33 + which, :] = theta
        return to_column(theta), to_column(scale)

    wait_all(field_row, vec_recv.at[0, 1])
    field_r = unpacked(field_row)
    mirror_products(field_r, 0)
    wait_all(field_col, vec_recv.at[0, 0])
    field_c = [unpacked(field_col.at[h]) for h in range(2)]
    direct_products(field_c, 0)
    image_p = summed(0) + energy_part
    image_out[0:GROUP] = image_p
    image_own = unpack_own(image_p)
    share_stats(field_own, image_own, 0)
    row_put(image_out, image_row, vec_send.at[1, 1], vec_recv.at[1, 1])
    col_put(image_out, image_col, vec_send.at[1, 0], vec_recv.at[1, 0])
    relay_stats(0)
    wait_all(image_row, vec_recv.at[1, 1])
    wait_all(image_col, vec_recv.at[1, 0])

    image_r, ready_r = unpacked(image_row), unpacked(image_row, GROUP)
    image_c = [unpacked(image_col.at[h]) for h in range(2)]
    ready_c = [unpacked(image_col.at[h], GROUP) for h in range(2)]
    theta, scale = merge_stats(0)
    mix = [mix_ref[i, 0:NVEC] for i in range(2)]

    def following(field, image, ready):
        scaled = (image - theta * field) * scale
        return ready + mixed(mix[0], [(1, scaled)])

    mirror_products(following(field_r, image_r, ready_r), 1)
    direct_products([following(field_c[h], image_c[h], ready_c[h]) for h in range(2)], 1)
    scaled = (image_own - theta * field_own) * scale
    search_own = mixed(mix[0], [(1, scaled), (2, search_own)])
    field_own = mixed(mix[0], [(0, field_own)]) + search_own
    image_own = unpack_own(summed(1)) + energy * field_own
    share_stats(field_own, image_own, 1)
    search_part = mixed(mix[1], [(2, search_own)])
    field_part = mixed(mix[1], [(0, field_own)])
    relay_stats(1)
    theta, scale = merge_stats(1)
    scaled = (image_own - theta * field_own) * scale
    search_own = search_part + mixed(mix[1], [(1, scaled)])
    out_ref[0:NVEC, :] = field_part + search_own
    out_ref[NVEC : 2 * NVEC, :] = search_own

    def drain(sem, ref, whole, diagonal):
        if not diagonal:
            wait_all(ref.at[pl.ds(0, whole)], sem)
        else:
            @pl.when(on_diag)
            def _():
                wait_all(ref.at[pl.ds(0, whole - 1)], sem)

            @pl.when(jnp.logical_not(on_diag))
            def _():
                wait_all(ref.at[pl.ds(0, whole)], sem)

    def drain_wide():
        wait_all(image_col.at[0], vec_send.at[1, 0])

        @pl.when(on_diag)
        def _():
            wait_all(image_col.at[1, pl.ds(0, COLS - 1)], vec_send.at[1, 0])

        @pl.when(jnp.logical_not(on_diag))
        def _():
            wait_all(image_col.at[1], vec_send.at[1, 0])

    spare = sums.at[0]
    drain(vec_send.at[0, 0], spare, ROWS, True)
    drain(vec_send.at[0, 1], spare, COLS - 1, False)
    wide = image_col.at[0]
    drain(vec_send.at[1, 1], wide, COLS - 1, False)
    drain_wide()
    for which in range(2):
        drain(sums_send.at[which, 0], spare, 2 * COLS, True)
        drain(sums_send.at[which, 1], spare, COLS - 1, False)
    for which in range(2):
        drain(stat_send.at[which, 0], spare, COLS - 1, False)
        drain(stat_send.at[which, 1], spare, ROWS - 1, False)


def split_out(all_ref, field_ref, search_ref, theta_ref):
    field_ref[...] = all_ref[0:NVEC, 0:QUARTER]
    search_ref[...] = all_ref[NVEC : 2 * NVEC, 0:QUARTER]
    theta_ref[...] = all_ref[32:34, 0:NVEC]


def body(tiles, energy, vectors, previous, coefs, irrep_of_unit, coupled):
    f32 = jnp.float32
    dma = pltpu.SemaphoreType.DMA
    vmem = pl.BlockSpec(memory_space=pltpu.VMEM)
    piece = (GROUP, LANES)
    everything = pl.pallas_call(
        kernel,
        out_shape=jax.ShapeDtypeStruct((40, LANES), f32),
        in_specs=[pl.BlockSpec(memory_space=pl.ANY)] * 7,
        out_specs=vmem,
        scratch_shapes=[
            pltpu.VMEM((NVEC, QUARTER), f32),
            pltpu.VMEM((NVEC, QUARTER), f32),
            pltpu.VMEM((1, QUARTER), f32),
            pltpu.VMEM(coefs.shape, f32),
            pltpu.SMEM(irrep_of_unit.shape, jnp.int32),
            pltpu.SMEM(coupled.shape, jnp.int32),
            pltpu.VMEM((SEG, 2, SEG), jnp.bfloat16),
            pltpu.VMEM((2, SEG, SEG), jnp.bfloat16),
            pltpu.VMEM((40, LANES), f32),
            pltpu.VMEM((2, LANES, LANES), f32),
            pltpu.VMEM(piece, f32),
            pltpu.VMEM((2 * GROUP, LANES), f32),
            pltpu.VMEM((COLS, *piece), f32),
            pltpu.VMEM((2, COLS, *piece), f32),
            pltpu.VMEM((COLS, 2 * GROUP, LANES), f32),
            pltpu.VMEM((2, COLS, 2 * GROUP, LANES), f32),
            pltpu.VMEM((2, COLS, *piece), f32),
            pltpu.VMEM((2, 2, COLS, *piece), f32),
            pltpu.VMEM((2, COLS + ROWS, *piece), f32),
            pltpu.VMEM((2, 2, *piece), f32),
            pltpu.VMEM((2, COLS, *piece), f32),
            pltpu.VMEM((2, ROWS, *piece), f32),
            dma,
            dma((6,)), dma((2, 2)), dma((2, 2)), dma((2, 2)), dma((2,)), dma((2, 2)), dma((2, 2)),
        ],
        compiler_params=pltpu.CompilerParams(collective_id=0, has_side_effects=True),
        name="lobpcg",
    )(tiles, energy[None, :], vectors, previous, coefs, irrep_of_unit, coupled)
    return pl.pallas_call(
        split_out,
        out_shape=(
            jax.ShapeDtypeStruct((NVEC, QUARTER), f32),
            jax.ShapeDtypeStruct((NVEC, QUARTER), f32),
            jax.ShapeDtypeStruct((2, NVEC), f32),
        ),
        in_specs=[vmem],
        out_specs=(vmem, vmem, vmem),
        name="split",
    )(everything)


def solution(mesh):
    placed = (
        P("row", None, "col"),
        P(("row", "col")),
        P(None, ("row", "col")),
        P(None, ("row", "col")),
        P(),
        P(),
        P(),
    )
    return jax.shard_map(
        body,
        mesh=mesh,
        in_specs=placed,
        out_specs=(P(None, ("row", "col")), P(None, ("row", "col")), P()),
        check_vma=False,
    )
```

time: 77.1 us -> 75.9 us (0.984)
  Pallas kernels: 76.2 us -> 75.1 us
    pallas_call x1, Pallas kernels: 74.9 us -> 73.7 us  [body(): pl.pallas_call(kernel, out_shape=jax.ShapeDtypeStruct((40, LANES), f32),...]
where the time goes in v3:
time: 75.9 us; the launch traced here: 75.7 us
  Pallas kernels  75.1 us (99%)
    pallas_call x1, Pallas kernels, body(): pl.pallas_call(kernel, out_shape=jax.ShapeDtypeStruct((40, LANES), f32),...  73.7 us

profile of v3, /device:TPU:1, one launch (start us, length us, event | category | flops | bytes accessed | tf_op | source)
XLA Modules:
  0.0 75.7 jit_solution(10063560426623523732)
XLA Ops:
  0.6 73.7 %lobpcg.1.all_ref = f32[40,128]{1,0:T(8,128)} custom-call(bf16[512,2,512]{2,1,0:T(2,128)(2,1)} %tiles_hbm.1, f32[1,32]{1,0:T(1,128)} %bitcast.1, f32[16,32]{1,0:T(8,128)} %vectors_hbm.1, f32[16,32]{1,0:T(8,128)} %previous_hbm.1, f32[2,3,16,16]{3,2,1,0:T(8,128)} %coefs_hbm.1, s32[256]{0:T(256)} %irrep_hbm.1, s32[64,64]{1,0:T(8,128)} %coupled_hbm.1), custom_call_target="tpu_custom_call" | custom-call | tf_op jit(solution)/shard_map/lobpcg/pallas_call | solution.py:418
  74.4 1.3 %split.1 = (f32[16,32]{1,0:T(8,128)}, f32[16,32]{1,0:T(8,128)}, f32[2,16]{1,0:T(2,128)}) custom-call(f32[40,128]{1,0:T(8,128)} %lobpcg.1.all_ref), custom_call_target="tpu_custom_call" | custom-call | tf_op jit(solution)/shard_map/split/pallas_call | solution.py:452

commit v4 on v3

--- a/solution.py
+++ b/solution.py
@@ -127,17 +127,16 @@
         def _():
             pl.semaphore_signal(barrier, inc=1, device_id=(r, c), device_id_type=MESH)
 
-    def greet_partners(k, carry):
-        greet(lax.rem(k, 2) * COLS + col, k // 2)
-        greet(k, home)
+    def greet_sources(k, carry):
+        greet(lax.rem(k, 2) * COLS + col, 2 * (k // 2))
         return carry
 
     def greet_row(k, carry):
-        greet(row, k)
+        greet(row, 2 * k)
         return carry
 
-    lax.fori_loop(0, ROWS, greet_partners, 0)
-    lax.fori_loop(0, COLS, greet_row, 0)
+    lax.fori_loop(0, COLS, greet_sources, 0)
+    lax.fori_loop(0, COLS // 2, greet_row, 0)
 
     loads = []
     for i, (src, dst) in enumerate((
@@ -189,7 +188,17 @@
         square = mix_ref[i]
         mix_ref[i] = square.T
 
-    pl.semaphore_wait(barrier, 15 + 64 - 2 * on_diag.astype(jnp.int32))
+    first = core == 0
+    skipped = jnp.logical_and(on_diag, first).astype(jnp.int32)
+
+    @pl.when(first)
+    def _():
+        pl.semaphore_wait(barrier, 15 + 32 - skipped)
+        pl.semaphore_signal(barrier, inc=1, device_id=(row, col + 1), device_id_type=MESH)
+
+    @pl.when(jnp.logical_not(first))
+    def _():
+        pl.semaphore_wait(barrier, 1)
 
     def put(src, dst, send, recv, r, c):
         mine = is_self(r, c)
@@ -223,18 +232,22 @@
     image_out[GROUP:] = pack_own(mixed(mix_ref[0, 0:NVEC], [(0, field_own), (2, search_own)]))
     energy_part = pack_own(energy * field_own)
 
-    def mirror_products(vectors, which):
+    def mirror_products(vectors, which, first=None):
         narrow = vectors.astype(jnp.bfloat16)
         for h in range(2):
             mirror = jnp.dot(narrow, masked[h], preferred_element_type=jnp.float32)
             store_packed(mirror_out.at[which, h], mirror)
 
-            def mirror_put(k, carry):
-                j = lax.rem(k + row, COLS)
-                put(mirror_out.at[which, h, j], sums.at[which, COLS + row], sums_send.at[which, 0], sums_recv.at[which], COLS * h + col, j)
-                return carry
-
-            lax.fori_loop(0, COLS, mirror_put, 0)
+        if first is not None:
+            first()
+
+        def mirror_put(k, carry):
+            h = k // COLS
+            j = lax.rem(k + row, COLS)
+            put(mirror_out.at[which, h, j], sums.at[which, COLS + row], sums_send.at[which, 0], sums_recv.at[which], COLS * h + col, j)
+            return carry
+
+        lax.fori_loop(0, 2 * COLS, mirror_put, 0)
 
     def direct_products(vectors, which):
         direct = jnp.zeros((NVEC, SEG), jnp.float32)
@@ -327,8 +340,7 @@
 
     wait_all(field_row, vec_recv.at[0, 1])
     field_r = unpacked(field_row)
-    mirror_products(field_r, 0)
-    wait_all(field_col, vec_recv.at[0, 0])
+    mirror_products(field_r, 0, lambda: wait_all(field_col, vec_recv.at[0, 0]))
     field_c = [unpacked(field_col.at[h]) for h in range(2)]
     direct_products(field_c, 0)
     image_p = summed(0) + energy_part

time: 75.9 us -> 75.6 us (level)
  no operation moved by 1% of the time
where the time goes in v4:
time: 75.6 us; the launch traced here: 75.4 us
  Pallas kernels  74.7 us (99%)
    pallas_call x1, Pallas kernels, body(): pl.pallas_call(kernel, out_shape=jax.ShapeDtypeStruct((40, LANES), f32),...  73.4 us

profile of v4, /device:TPU:1, one launch (start us, length us, event | category | flops | bytes accessed | tf_op | source)
XLA Modules:
  0.0 75.4 jit_solution(11919174383040854656)
XLA Ops:
  0.6 73.4 %lobpcg.1.all_ref = f32[40,128]{1,0:T(8,128)} custom-call(bf16[512,2,512]{2,1,0:T(2,128)(2,1)} %tiles_hbm.1, f32[1,32]{1,0:T(1,128)} %bitcast.1, f32[16,32]{1,0:T(8,128)} %vectors_hbm.1, f32[16,32]{1,0:T(8,128)} %previous_hbm.1, f32[2,3,16,16]{3,2,1,0:T(8,128)} %coefs_hbm.1, s32[256]{0:T(256)} %irrep_hbm.1, s32[64,64]{1,0:T(8,128)} %coupled_hbm.1), custom_call_target="tpu_custom_call" | custom-call | tf_op jit(solution)/shard_map/lobpcg/pallas_call | solution.py:430
  74.0 1.3 %split.1 = (f32[16,32]{1,0:T(8,128)}, f32[16,32]{1,0:T(8,128)}, f32[2,16]{1,0:T(2,128)}) custom-call(f32[40,128]{1,0:T(8,128)} %lobpcg.1.all_ref), custom_call_target="tpu_custom_call" | custom-call | tf_op jit(solution)/shard_map/split/pallas_call | solution.py:464
